TPU v7x, 256 devices: a whole 4x4x8 slice. The times are simulated.
256 devices in a mesh: gx: 32 (over y, x, core), gy: 8 (over z).
Axes of the slice: x: 4, y: 4, z: 8, core: 2. Of those that a mesh axis runs over, the one named last changes fastest.
Arguments:
- velocity: float32 [2, 3, 1536, 1024], P(None, None, 'gx', 'gy'), may hold values from -6 to 6
- stretch: float32 [1024], replicated, may hold values from 0.7 to 1.4
- second_metric: float32 [1024], replicated, may hold values from -1 to 1
Outputs:
- section_rhs: float32 [2, 3, 1536, 1024], P(None, None, 'gx', 'gy')
All inputs are finite; a program needn't handle non-finite values.
Results may differ from a plain program's by a relative error of at most 0.000054.
Values sent between devices are 32-bit elements; how exact they have to be, the bound alone decides.
A program may use at most 64 MiB of HBM per device.

v0:
```python
import functools

import jax
import jax.numpy as jnp
import numpy as np
from jax import lax
from jax.experimental import pallas as pl
from jax.experimental.pallas import tpu as pltpu
from jax.sharding import PartitionSpec as P

MESH = pl.DeviceIdType.MESH
HIGHEST = lax.Precision.HIGHEST

C1, C2 = 1.0 / 3.0, 2.0 / 11.0
R1 = (-1.0 + np.sqrt(1.0 - 4.0 * C1 * C1)) / (2.0 * C1)
R2 = (-1.0 + np.sqrt(1.0 - 4.0 * C2 * C2)) / (2.0 * C2)
K1 = 1.0 / (1.0 + 2.0 * C1 * R1)
K2 = 1.0 / (1.0 + 2.0 * C2 * R2)
G1 = (25.0 / 36.0) * K1 * (R1 - 1.0 / R1)
G2 = -(75.0 / 88.0) * 7.5 * K2
NEAR1 = -1.0 / 12.0
NEAR2 = 3.0 / 8.0
ZERO2 = (75.0 / 88.0) * (5.5 - 7.5 * K2) - 0.75


def x_tables(rows):
    d = np.arange(rows)[:, None] - np.arange(rows)[None, :]
    first = G1 * np.sign(d) * R1 ** np.abs(d) + NEAR1 * np.where(np.abs(d) == 1, np.sign(d), 0)
    second = G2 * R2 ** np.abs(d) * (d != 0) + NEAR2 * (np.abs(d) == 1) + ZERO2 * (d == 0)
    inner = np.concatenate([first, 0.5 * second])
    up = np.arange(1, rows + 1)
    down = rows - np.arange(rows)
    powers = np.stack([R1**up, R1**down, R2**up, R2**down])
    powers = np.broadcast_to(powers[:, :, None], (4, rows, 128))
    return inner.astype(np.float32), powers.astype(np.float32)


def y_tables(total, width):
    rows = np.arange(total)
    near = (rows == 1) | (rows == total - 2)
    edge = (rows == 0) | (rows == total - 1)
    bands = (
        np.where(edge, 0.0, np.where(near, 0.25, C1)),
        np.where(edge, 0.0, np.where(near, 0.1, C2)),
    )
    b1 = np.zeros((total, total))
    b2 = np.zeros((total, total))
    for j in range(2, total - 2):
        b1[j, j - 2 : j + 3] = [-1 / 36, -7 / 9, 0.0, 7 / 9, 1 / 36]
        b2[j, j - 2 : j + 3] = [3 / 44, 12 / 11, -24 / 11 - 6 / 44, 12 / 11, 3 / 44]
    for j in (1, total - 2):
        b1[j, j - 1 : j + 2] = [-0.75, 0.0, 0.75]
        b2[j, j - 1 : j + 2] = [1.2, -2.4, 1.2]
    b1[0, :3] = [-1.5, 2.0, -0.5]
    b1[-1, -3:] = [0.5, -2.0, 1.5]
    b2[0, :4] = [2.0, -5.0, 4.0, -1.0]
    b2[-1, -4:] = [-1.0, 4.0, -5.0, 2.0]
    whole = []
    for band, b in zip(bands, (b1, b2)):
        a = np.eye(total) + np.diag(band[1:], -1) + np.diag(band[:-1], 1)
        whole.append(np.linalg.solve(a, b))
    blocks = total // width
    inner = np.zeros((blocks, width, 2 * width))
    for q in range(blocks):
        own = slice(q * width, (q + 1) * width)
        inner[q, :, :width] = whole[0][own, own].T
        inner[q, :, width:] = 0.5 * whole[1][own, own].T
    up = np.arange(1, width + 1)
    down = width - np.arange(width)
    gather = np.zeros((8, width))
    gather[0], gather[1], gather[2, -1] = R1**down, R2**down, 1.0
    gather[3], gather[4], gather[5, 0] = R1**up, R2**up, 1.0
    spread = np.zeros((16, 2 * width))
    spread[0, :width] = G1 * R1 ** (up - 1)
    spread[1, width:] = 0.5 * G2 * R2 ** (up - 1)
    spread[2, 0], spread[2, width] = NEAR1, 0.5 * NEAR2
    spread[11, :width] = -G1 * R1 ** (down - 1)
    spread[12, width:] = 0.5 * G2 * R2 ** (down - 1)
    spread[13, width - 1], spread[13, 2 * width - 1] = -NEAR1, 0.5 * NEAR2
    small = np.finfo(np.float32).tiny
    return [
        np.where(np.abs(t) < small, 0.0, t).astype(np.float32)
        for t in (inner, gather, spread)
    ]


def kernel(
    nx, ny, vel, powers, x_inner, y_inner, gather, spread, stretch, metric, out,
    f, pw, wx, wy, ga, sp, st, sm, z, xs, ys, xr, xf, yr,
    load_sem, store_sem, send_sem, recv_sem,
):
    gx = lax.axis_index("gx")
    gy = lax.axis_index("gy")
    rows = f.shape[1]
    width = f.shape[2]
    comps = f.shape[0]

    loads = [
        pltpu.make_async_copy(src, dst, load_sem.at[n])
        for n, (src, dst) in enumerate(
            (
                (vel, f), (powers, pw), (gather, ga), (x_inner, wx),
                (y_inner.at[gy], wy), (spread, sp), (stretch, st), (metric, sm),
            )
        )
    ]
    for copy in loads:
        copy.start()

    right, left = lax.rem(gx + 1, nx), lax.rem(gx + nx - 1, nx)
    right2, left2 = lax.rem(gx + 2, nx), lax.rem(gx + nx - 2, nx)
    barrier = pltpu.get_barrier_semaphore()
    for peer in (right, left, right2, left2):
        pl.semaphore_signal(barrier, inc=1, device_id=(peer, gy), device_id_type=MESH)

    @pl.when(gy > 0)
    def _():
        pl.semaphore_signal(barrier, inc=1, device_id=(gx, gy - 1), device_id_type=MESH)

    @pl.when(gy < ny - 1)
    def _():
        pl.semaphore_signal(barrier, inc=1, device_id=(gx, gy + 1), device_id_type=MESH)

    for copy in loads[:2]:
        copy.wait()
    for c in range(comps):
        fc = f[c]
        xs[0, c : c + 1] = jnp.sum(fc * pw[1], axis=0, keepdims=True)
        xs[0, 8 + c : 9 + c] = jnp.sum(fc * pw[3], axis=0, keepdims=True)
        xs[0, 16 + c : 17 + c] = fc[rows - 1 : rows]
        xs[1, c : c + 1] = jnp.sum(fc * pw[0], axis=0, keepdims=True)
        xs[1, 8 + c : 9 + c] = jnp.sum(fc * pw[2], axis=0, keepdims=True)
        xs[1, 16 + c : 17 + c] = fc[0:1]

    beside_y = jnp.minimum(gy, 1) + jnp.minimum(ny - 1 - gy, 1)
    pl.semaphore_wait(barrier, 4 + beside_y)

    def send(n, src, dst, peer):
        return pltpu.make_async_remote_copy(
            src_ref=src, dst_ref=dst, send_sem=send_sem.at[n], recv_sem=recv_sem.at[n],
            device_id=peer, device_id_type=MESH,
        )

    x_copies = [
        send(0, xs.at[0], xr.at[0], (right, gy)),
        send(1, xs.at[1], xr.at[1], (left, gy)),
        send(2, xs.at[0, 0:16], xf.at[0], (right2, gy)),
        send(3, xs.at[1, 0:16], xf.at[1], (left2, gy)),
    ]
    for copy in x_copies:
        copy.start()

    loads[2].wait()
    flat = f[...].reshape(comps * rows, width)
    ys[...] = lax.dot_general(
        ga[...], flat, (((1,), (1,)), ((), ())), precision=HIGHEST,
        preferred_element_type=jnp.float32,
    )
    y_right = send(4, ys, yr.at[0:8], (gx, gy + 1))
    y_left = send(5, ys, yr.at[8:16], (gx, gy - 1))

    @pl.when(gy < ny - 1)
    def _():
        y_right.start()

    @pl.when(gy > 0)
    def _():
        y_left.start()

    @pl.when(gy == 0)
    def _():
        yr[0:8] = jnp.zeros((8, comps * rows), jnp.float32)

    @pl.when(gy == ny - 1)
    def _():
        yr[8:16] = jnp.zeros((8, comps * rows), jnp.float32)

    for copy in loads[3:]:
        copy.wait()
    side = jnp.concatenate([f[c] for c in range(comps)], axis=1)
    own_x = jnp.dot(wx[...], side, precision=HIGHEST, preferred_element_type=jnp.float32)
    own_y = jnp.dot(flat, wy[...], precision=HIGHEST, preferred_element_type=jnp.float32)
    inv = 1.0 / st[pl.ds(gy, 1), :]
    inv2 = inv * inv
    bend = -0.5 * sm[pl.ds(gy, 1), :] * inv2 * inv

    def along_y(part, c):
        block = part[c * rows : (c + 1) * rows]
        v = f[3 * (c // 3) + 1]
        return block[:, :width] * (bend - v * inv) + block[:, width:] * inv2

    for c in range(comps):
        lanes = slice(c * width, (c + 1) * width)
        u = f[3 * (c // 3)]
        z[c] = own_x[rows:, lanes] - u * own_x[:rows, lanes] + along_y(own_y, c)

    for copy in x_copies:
        copy.wait_recv()
    far1 = np.float32(R1**rows)
    far2 = np.float32(R2**rows)
    left1 = (xr[0, 0:8] + far1 * xf[0, 0:8]) * np.float32(G1 / R1)
    left2_ = (xr[0, 8:16] + far2 * xf[0, 8:16]) * np.float32(0.5 * G2 / R2)
    right1 = (xr[1, 0:8] + far1 * xf[1, 0:8]) * np.float32(-G1 / R1)
    right2_ = (xr[1, 8:16] + far2 * xf[1, 8:16]) * np.float32(0.5 * G2 / R2)
    for c in range(comps):
        row = slice(c, c + 1)
        u = f[3 * (c // 3)]
        first = pw[0] * left1[row] + pw[1] * right1[row]
        second = pw[2] * left2_[row] + pw[3] * right2_[row]
        z[c] = z[c] + (second - u * first)
        near = 0.5 * NEAR2 - NEAR1 * u[0:1]
        z[c, 0:1] = z[c, 0:1] + near * xr[0, 16 + c : 17 + c]
        near = 0.5 * NEAR2 + NEAR1 * u[rows - 1 : rows]
        z[c, rows - 1 : rows] = z[c, rows - 1 : rows] + near * xr[1, 16 + c : 17 + c]

    @pl.when(gy > 0)
    def _():
        y_right.wait_recv()

    @pl.when(gy < ny - 1)
    def _():
        y_left.wait_recv()

    beside = lax.dot_general(
        yr[...], sp[...], (((0,), (0,)), ((), ())), precision=HIGHEST,
        preferred_element_type=jnp.float32,
    )
    stores = []
    for c in range(comps):
        z[c] = z[c] + along_y(beside, c)
        stores.append(pltpu.make_async_copy(z.at[c], out.at[c], store_sem.at[c]))
        stores[-1].start()

    for copy in x_copies:
        copy.wait_send()

    @pl.when(gy < ny - 1)
    def _():
        y_right.wait_send()

    @pl.when(gy > 0)
    def _():
        y_left.wait_send()

    for copy in stores:
        copy.wait()


def solution(mesh):
    nx, ny = mesh.shape["gx"], mesh.shape["gy"]

    def shards(velocity, stretch, second_metric):
        planes, parts, rows, width = velocity.shape
        comps = planes * parts
        x_inner, powers = x_tables(rows)
        y_inner, gather, spread = y_tables(ny * width, width)
        hbm = pl.BlockSpec(memory_space=pltpu.MemorySpace.HBM)
        f32 = jnp.float32
        out = pl.pallas_call(
            functools.partial(kernel, nx, ny),
            out_shape=jax.ShapeDtypeStruct((comps, rows, width), f32),
            in_specs=[hbm] * 8,
            out_specs=hbm,
            scratch_shapes=[
                pltpu.VMEM((comps, rows, width), f32),
                pltpu.VMEM((4, rows, 128), f32),
                pltpu.VMEM((2 * rows, rows), f32),
                pltpu.VMEM((width, 2 * width), f32),
                pltpu.VMEM((8, width), f32),
                pltpu.VMEM((16, 2 * width), f32),
                pltpu.VMEM((ny, width), f32),
                pltpu.VMEM((ny, width), f32),
                pltpu.VMEM((comps, rows, width), f32),
                pltpu.VMEM((2, 24, width), f32),
                pltpu.VMEM((8, comps * rows), f32),
                pltpu.VMEM((2, 24, width), f32),
                pltpu.VMEM((2, 16, width), f32),
                pltpu.VMEM((16, comps * rows), f32),
                pltpu.SemaphoreType.DMA((8,)),
                pltpu.SemaphoreType.DMA((comps,)),
                pltpu.SemaphoreType.DMA((6,)),
                pltpu.SemaphoreType.DMA((6,)),
            ],
            compiler_params=pltpu.CompilerParams(collective_id=0, has_side_effects=True),
        )(
            velocity.reshape(comps, rows, width),
            jnp.asarray(powers), jnp.asarray(x_inner), jnp.asarray(y_inner),
            jnp.asarray(gather), jnp.asarray(spread),
            stretch.reshape(ny, width), second_metric.reshape(ny, width),
        )
        return out.reshape(velocity.shape)

    return jax.shard_map(
        shards,
        mesh=mesh,
        in_specs=(P(None, None, "gx", "gy"), P(), P()),
        out_specs=P(None, None, "gx", "gy"),
        check_vma=False,
    )
```

profile of v0, /device:TPU:96, one launch (start us, length us, event | category | flops | bytes accessed | tf_op | source)
XLA Modules:
  0.0 13.4 jit_solution(15998561201196018590)
XLA Ops:
  0.0 11.8 %shard_map.82 = f32[6,48,128]{2,1,0:T(8,128)} custom-call(f32[6,48,128]{2,1,0:T(8,128)} %bitcast.5, f32[4,48,128]{2,1,0:T(8,128)} %constant.10.clone.powers, f32[96,48]{1,0:T(8,128)} %constant.11.clone.x_inner, f32[8,128,256]{2,1,0:T(8,128)} %constant.12.clone.y_inner, f32[8,128]{1,0:T(8,128)} %constant.13.clone.gather, f32[16,256]{1,0:T(8,128)} %constant.14.clone.spread, ...), custom_call_target="tpu_custom_call" | custom-call | tf_op jit(solution)/shard_map/pallas_call | solution.py:259
  11.8 1.6 %copy.10 = f32[2,3,48,128]{3,2,1,0:T(8,128)} copy(f32[2,3,48,128]{3,2,1,0:T(8,128)} %bitcast.4) | data formatting | bytes 294912
where the time goes:
time: 13.5 us; the launch traced here: 13.4 us
  Pallas kernels  11.8 us (87%)
  local copies, waits for them, and re-layouts  1.58 us (12%)
    pallas_call x1, Pallas kernels, shards(): pl.pallas_call(functools.partial(kernel, nx, ny), out_shape=jax.ShapeDtyp...  11.8 us
    unnamed x1, local copies, waits for them, and re-layouts  1.58 us

commit v1 on v0

v1 whole, which is shorter than its diff:
```python
import functools

import jax
import jax.numpy as jnp
import numpy as np
from jax import lax
from jax.experimental import pallas as pl
from jax.experimental.pallas import tpu as pltpu
from jax.sharding import PartitionSpec as P

MESH = pl.DeviceIdType.MESH
HIGHEST = lax.Precision.HIGHEST

C1, C2 = 1.0 / 3.0, 2.0 / 11.0
R1 = (-1.0 + np.sqrt(1.0 - 4.0 * C1 * C1)) / (2.0 * C1)
R2 = (-1.0 + np.sqrt(1.0 - 4.0 * C2 * C2)) / (2.0 * C2)
K1 = 1.0 / (1.0 + 2.0 * C1 * R1)
K2 = 1.0 / (1.0 + 2.0 * C2 * R2)
G1 = (25.0 / 36.0) * K1 * (R1 - 1.0 / R1)
G2 = -(75.0 / 88.0) * 7.5 * K2
NEAR1 = -1.0 / 12.0
NEAR2 = 3.0 / 8.0
ZERO2 = (75.0 / 88.0) * (5.5 - 7.5 * K2) - 0.75


def x_tables(rows):
    d = np.arange(rows)[:, None] - np.arange(rows)[None, :]
    first = G1 * np.sign(d) * R1 ** np.abs(d) + NEAR1 * np.where(np.abs(d) == 1, np.sign(d), 0)
    second = G2 * R2 ** np.abs(d) * (d != 0) + NEAR2 * (np.abs(d) == 1) + ZERO2 * (d == 0)
    inner = np.concatenate([first, 0.5 * second])
    return inner.astype(np.float32)


def y_tables(total, width):
    rows = np.arange(total)
    near = (rows == 1) | (rows == total - 2)
    edge = (rows == 0) | (rows == total - 1)
    bands = (
        np.where(edge, 0.0, np.where(near, 0.25, C1)),
        np.where(edge, 0.0, np.where(near, 0.1, C2)),
    )
    b1 = np.zeros((total, total))
    b2 = np.zeros((total, total))
    for j in range(2, total - 2):
        b1[j, j - 2 : j + 3] = [-1 / 36, -7 / 9, 0.0, 7 / 9, 1 / 36]
        b2[j, j - 2 : j + 3] = [3 / 44, 12 / 11, -24 / 11 - 6 / 44, 12 / 11, 3 / 44]
    for j in (1, total - 2):
        b1[j, j - 1 : j + 2] = [-0.75, 0.0, 0.75]
        b2[j, j - 1 : j + 2] = [1.2, -2.4, 1.2]
    b1[0, :3] = [-1.5, 2.0, -0.5]
    b1[-1, -3:] = [0.5, -2.0, 1.5]
    b2[0, :4] = [2.0, -5.0, 4.0, -1.0]
    b2[-1, -4:] = [-1.0, 4.0, -5.0, 2.0]
    whole = []
    for band, b in zip(bands, (b1, b2)):
        a = np.eye(total) + np.diag(band[1:], -1) + np.diag(band[:-1], 1)
        whole.append(np.linalg.solve(a, b))
    blocks = total // width
    inner = np.zeros((blocks, width, 2 * width))
    for q in range(blocks):
        own = slice(q * width, (q + 1) * width)
        inner[q, :, :width] = whole[0][own, own].T
        inner[q, :, width:] = 0.5 * whole[1][own, own].T
    up = np.arange(1, width + 1)
    down = width - np.arange(width)
    gather = np.zeros((8, width))
    gather[0], gather[1], gather[2, -1] = R1**down, R2**down, 1.0
    gather[3], gather[4], gather[5, 0] = R1**up, R2**up, 1.0
    spread = np.zeros((16, 2 * width))
    spread[0, :width] = G1 * R1 ** (up - 1)
    spread[1, width:] = 0.5 * G2 * R2 ** (up - 1)
    spread[2, 0], spread[2, width] = NEAR1, 0.5 * NEAR2
    spread[11, :width] = -G1 * R1 ** (down - 1)
    spread[12, width:] = 0.5 * G2 * R2 ** (down - 1)
    spread[13, width - 1], spread[13, 2 * width - 1] = -NEAR1, 0.5 * NEAR2
    small = np.finfo(np.float32).tiny
    return [
        np.where(np.abs(t) < small, 0.0, t).astype(np.float32)
        for t in (inner, gather, spread)
    ]


FAR = True


def kernel(
    nx, ny, vel, tables, stretch, metric, out, f, late, xs, ys, xr, yr,
    load_sem, x_sem, y_sem,
):
    gx = lax.axis_index("gx")
    gy = lax.axis_index("gy")
    comps, rows, width = f.shape
    steps = rows // 8
    t_rows = tables.shape[1]

    def row_copy(n):
        part = slice(n * comps // 3, (n + 1) * comps // 3)
        return pltpu.make_async_copy(vel.at[part], f.at[part], load_sem.at[0])

    for n in range(3):
        row_copy(n).start()

    odd = lax.rem(gx, 2)
    side = 2 * odd - 1
    outer, partner = lax.rem(gx + side + nx, nx), gx - side
    far_outer, far_partner = lax.rem(gx + 2 * side + nx, nx), lax.rem(gx - 2 * side + nx, nx)
    peers = (outer, partner, far_outer, far_partner) if FAR else (outer, partner)
    barrier = pltpu.get_barrier_semaphore()
    for peer in peers:
        pl.semaphore_signal(barrier, inc=1, device_id=(peer, gy), device_id_type=MESH)

    @pl.when(gy > 0)
    def _():
        pl.semaphore_signal(barrier, inc=1, device_id=(gx, gy - 1), device_id_type=MESH)

    @pl.when(gy < ny - 1)
    def _():
        pl.semaphore_signal(barrier, inc=1, device_id=(gx, gy + 1), device_id_type=MESH)

    low, high = jnp.minimum(gy, 1), jnp.minimum(ny - 1 - gy, 1)
    kind = low + 1 - high
    pltpu.make_async_copy(tables.at[kind], late.at[0:t_rows], load_sem.at[1]).start()
    pltpu.make_async_copy(stretch, late.at[t_rows : t_rows + ny], load_sem.at[1]).start()
    pltpu.make_async_copy(metric, late.at[t_rows + ny : t_rows + 2 * ny], load_sem.at[1]).start()

    place = lax.broadcasted_iota(jnp.int32, (8, width), 0)

    def powers(r, falling):
        tile = jnp.full((8, width), r ** (8 if falling else 1), jnp.float32)
        for n in range(1, 8):
            tile = jnp.where(place == n, np.float32(r ** (8 - n if falling else n + 1)), tile)
        return tile

    up1, down1 = powers(R1, False), powers(R1, True)
    up2, down2 = powers(R2, False), powers(R2, True)

    pltpu.make_async_copy(vel, f, load_sem.at[0]).wait()
    step1, step2 = np.float32(R1**8), np.float32(R2**8)

    def weighted(c, order, step, base):
        total = f[c, 8 * order[0] : 8 * order[0] + 8]
        for m in order[1:]:
            total = total * step + f[c, 8 * m : 8 * m + 8]
        return jnp.sum(total * base, axis=0, keepdims=True)

    rising, falling = list(range(steps)), list(range(steps))[::-1]
    to_right, to_left = 1 - odd, odd
    for c in range(comps):
        xs[to_right, c : c + 1] = weighted(c, rising, step1, down1)
        xs[to_right, 8 + c : 9 + c] = weighted(c, rising, step2, down2)
        xs[to_right, 16 + c : 17 + c] = f[c, rows - 1 : rows]
        xs[to_left, c : c + 1] = weighted(c, falling, step1, up1)
        xs[to_left, 8 + c : 9 + c] = weighted(c, falling, step2, up2)
        xs[to_left, 16 + c : 17 + c] = f[c, 0:1]

    pl.semaphore_wait(barrier, len(peers) + low + high)

    def send(src, dst, sem, peer):
        return pltpu.make_async_remote_copy(
            src_ref=src, dst_ref=dst, send_sem=sem.at[0], recv_sem=sem.at[1],
            device_id=peer, device_id_type=MESH,
        )

    send(xs.at[0], xr.at[0, 0:24], x_sem, (outer, gy)).start()
    if FAR:
        send(xs.at[1, 0:16], xr.at[0, 24:40], x_sem, (far_partner, gy)).start()
    send(xs.at[1], xr.at[1, 0:24], x_sem, (partner, gy)).start()
    if FAR:
        send(xs.at[0, 0:16], xr.at[1, 24:40], x_sem, (far_outer, gy)).start()

    pltpu.make_async_copy(late, late, load_sem.at[1]).wait()
    flat = f[...].reshape(comps * rows, width)
    ys[...] = lax.dot_general(
        late[0:8], flat, (((1,), (1,)), ((), ())), precision=HIGHEST,
        preferred_element_type=jnp.float32,
    )

    @pl.when(gy < ny - 1)
    def _():
        send(ys, yr.at[0:8], y_sem, (gx, gy + 1)).start()

    @pl.when(gy > 0)
    def _():
        send(ys, yr.at[8:16], y_sem, (gx, gy - 1)).start()

    @pl.when(gy == 0)
    def _():
        yr[0:8] = jnp.zeros((8, comps * rows), jnp.float32)

    @pl.when(gy == ny - 1)
    def _():
        yr[8:16] = jnp.zeros((8, comps * rows), jnp.float32)

    lanes = jnp.concatenate([f[c] for c in range(comps)], axis=1)
    own_x = jnp.dot(
        late[40 : 40 + 2 * rows][:, :rows], lanes, precision=HIGHEST,
        preferred_element_type=jnp.float32,
    )
    y_at = 40 + 2 * rows
    y_inner = jnp.concatenate([late[y_at + n * width : y_at + (n + 1) * width] for n in range(2)], axis=1)
    own_y = jnp.dot(flat, y_inner, precision=HIGHEST, preferred_element_type=jnp.float32)
    inv = 1.0 / late[pl.ds(t_rows + gy, 1), :]
    inv2 = inv * inv
    bend = -0.5 * late[pl.ds(t_rows + ny + gy, 1), :] * inv2 * inv

    def along_y(part, c):
        block = part[c * rows : (c + 1) * rows]
        v = f[3 * (c // 3) + 1]
        return block[:, :width] * (bend - v * inv) + block[:, width:] * inv2

    for c in range(comps):
        at = slice(c * width, (c + 1) * width)
        u = f[3 * (c // 3)]
        out[c] = own_x[rows:, at] - u * own_x[:rows, at] + along_y(own_y, c)

    inside = low + high == 2

    @pl.when(inside)
    def _():
        send(yr, yr, y_sem, (partner, gy)).wait_recv()

    @pl.when(jnp.logical_not(inside))
    def _():
        send(ys, ys, y_sem, (partner, gy)).wait_recv()

    spread = jnp.concatenate([late[8:24], late[24:40]], axis=1)
    beside = lax.dot_general(
        yr[...], spread, (((0,), (0,)), ((), ())), precision=HIGHEST,
        preferred_element_type=jnp.float32,
    )
    for c in range(comps):
        out[c] = out[c] + along_y(beside, c)

    send(xr, xr, x_sem, (partner, gy)).wait_recv()
    left, right = odd, 1 - odd
    far1, far2 = np.float32(R1**rows), np.float32(R2**rows)
    left1, left2 = xr[left, 0:8], xr[left, 8:16]
    right1, right2 = xr[right, 0:8], xr[right, 8:16]
    if FAR:
        left1, left2 = left1 + far1 * xr[left, 24:32], left2 + far2 * xr[left, 32:40]
        right1, right2 = right1 + far1 * xr[right, 24:32], right2 + far2 * xr[right, 32:40]
    left1, right1 = left1 * np.float32(G1 / R1), right1 * np.float32(-G1 / R1)
    left2, right2 = left2 * np.float32(0.5 * G2 / R2), right2 * np.float32(0.5 * G2 / R2)
    left_cell, right_cell = xr[left, 16:24], xr[right, 16:24]
    for c in range(comps):
        row = slice(c, c + 1)
        u = f[3 * (c // 3)]
        from_left1, from_right1 = up1 * left1[row], down1 * right1[row]
        from_left2, from_right2 = up2 * left2[row], down2 * right2[row]
        for m in range(steps):
            part = slice(8 * m, 8 * m + 8)
            lo, hi = np.float32(R1 ** (8 * m)), np.float32(R1 ** (rows - 8 - 8 * m))
            first = from_left1 * lo + from_right1 * hi
            lo, hi = np.float32(R2 ** (8 * m)), np.float32(R2 ** (rows - 8 - 8 * m))
            second = from_left2 * lo + from_right2 * hi
            if m == 0:
                cell = jnp.where(place == 0, left_cell[row], 0.0)
                first, second = first + NEAR1 * cell, second + 0.5 * NEAR2 * cell
            if m == steps - 1:
                cell = jnp.where(place == 7, right_cell[row], 0.0)
                first, second = first - NEAR1 * cell, second + 0.5 * NEAR2 * cell
            out[c, part] = out[c, part] + (second - u[part] * first)

    if FAR:
        send(xr, xr, x_sem, (partner, gy)).wait_send()
    else:
        send(xs, xs, x_sem, (partner, gy)).wait_send()

    @pl.when(inside)
    def _():
        send(yr, yr, y_sem, (partner, gy)).wait_send()

    @pl.when(jnp.logical_not(inside))
    def _():
        send(ys, ys, y_sem, (partner, gy)).wait_send()


def solution(mesh):
    nx, ny = mesh.shape["gx"], mesh.shape["gy"]

    def shards(velocity, stretch, second_metric):
        planes, parts, rows, width = velocity.shape
        comps = planes * parts
        x_inner = np.pad(x_tables(rows), ((0, 0), (0, width - rows)))
        y_inner, gather, spread = y_tables(ny * width, width)
        tables = np.stack(
            [
                np.concatenate(
                    [
                        gather, spread[:, :width], spread[:, width:], x_inner,
                        y_inner[q][:, :width], y_inner[q][:, width:],
                    ]
                )
                for q in (0, 1, ny - 1)
            ]
        )
        hbm = pl.BlockSpec(memory_space=pltpu.MemorySpace.HBM)
        f32 = jnp.float32
        out = pl.pallas_call(
            functools.partial(kernel, nx, ny),
            out_shape=pltpu.VMEM((comps, rows, width), f32),
            in_specs=[hbm] * 4,
            out_specs=pl.BlockSpec(memory_space=pltpu.VMEM),
            scratch_shapes=[
                pltpu.VMEM((comps, rows, width), f32),
                pltpu.VMEM((tables.shape[1] + 2 * ny, width), f32),
                pltpu.VMEM((2, 24, width), f32),
                pltpu.VMEM((8, comps * rows), f32),
                pltpu.VMEM((2, 40 if FAR else 24, width), f32),
                pltpu.VMEM((16, comps * rows), f32),
                pltpu.SemaphoreType.DMA((2,)),
                pltpu.SemaphoreType.DMA((2,)),
                pltpu.SemaphoreType.DMA((2,)),
            ],
            compiler_params=pltpu.CompilerParams(collective_id=0, has_side_effects=True),
        )(
            velocity.reshape(comps, rows, width), jnp.asarray(tables),
            stretch.reshape(ny, width), second_metric.reshape(ny, width),
        )
        return out.reshape(velocity.shape)

    return jax.shard_map(
        shards,
        mesh=mesh,
        in_specs=(P(None, None, "gx", "gy"), P(), P()),
        out_specs=P(None, None, "gx", "gy"),
        check_vma=False,
    )
```

time: 13.5 us -> 11.9 us (0.88)
  local copies, waits for them, and re-layouts: 1.58 us -> 0.66 us
  Pallas kernels: 11.8 us -> 11.1 us
    unnamed x1, local copies, waits for them, and re-layouts: 1.58 us -> 0.66 us
    pallas_call x1, Pallas kernels: 11.8 us -> 11.1 us  [shards(): pl.pallas_call(functools.partial(kernel, nx, ny), out_shape=pltpu.VMEM((c...]
where the time goes in v1:
time: 11.9 us; the launch traced here: 11.8 us
  Pallas kernels  11.1 us (93%)
  local copies, waits for them, and re-layouts  0.66 us (6%)
    pallas_call x1, Pallas kernels, shards(): pl.pallas_call(functools.partial(kernel, nx, ny), out_shape=pltpu.VMEM((c...  11.1 us
    unnamed x1, local copies, waits for them, and re-layouts  0.66 us

profile of v1, /device:TPU:96, one launch (start us, length us, event | category | flops | bytes accessed | tf_op | source)
XLA Modules:
  0.0 11.8 jit_solution(12852454934874682288)
XLA Ops:
  0.0 11.1 %shard_map.46 = f32[6,48,128]{2,1,0:T(8,128)S(1)} custom-call(f32[6,48,128]{2,1,0:T(8,128)} %bitcast.5, f32[3,392,128]{2,1,0:T(8,128)} %constant.2.clone.tables, f32[8,128]{1,0:T(8,128)} %bitcast.6, f32[8,128]{1,0:T(8,128)} %bitcast.7), custom_call_target="tpu_custom_call" | custom-call | tf_op jit(solution)/shard_map/pallas_call | solution.py:299
  11.1 0.7 %copy.6 = f32[2,3,48,128]{3,2,1,0:T(8,128)} copy(f32[2,3,48,128]{3,2,1,0:T(8,128)S(1)} %bitcast.4) | data formatting | bytes 294912

commit v2 on v1

--- a/solution.py
+++ b/solution.py
@@ -80,12 +80,9 @@
     ]
 
 
-FAR = True
-
-
 def kernel(
     nx, ny, vel, tables, stretch, metric, out, f, late, xs, ys, xr, yr,
-    load_sem, x_sem, y_sem,
+    sems, ready,
 ):
     gx = lax.axis_index("gx")
     gy = lax.axis_index("gy")
@@ -95,33 +92,32 @@
 
     def row_copy(n):
         part = slice(n * comps // 3, (n + 1) * comps // 3)
-        return pltpu.make_async_copy(vel.at[part], f.at[part], load_sem.at[0])
+        return pltpu.make_async_copy(vel.at[part], f.at[part], sems.at[0])
 
     for n in range(3):
         row_copy(n).start()
 
-    odd = lax.rem(gx, 2)
-    side = 2 * odd - 1
-    outer, partner = lax.rem(gx + side + nx, nx), gx - side
-    far_outer, far_partner = lax.rem(gx + 2 * side + nx, nx), lax.rem(gx - 2 * side + nx, nx)
-    peers = (outer, partner, far_outer, far_partner) if FAR else (outer, partner)
+    last = nx - 1
     barrier = pltpu.get_barrier_semaphore()
-    for peer in peers:
-        pl.semaphore_signal(barrier, inc=1, device_id=(peer, gy), device_id_type=MESH)
-
-    @pl.when(gy > 0)
-    def _():
-        pl.semaphore_signal(barrier, inc=1, device_id=(gx, gy - 1), device_id_type=MESH)
-
-    @pl.when(gy < ny - 1)
-    def _():
-        pl.semaphore_signal(barrier, inc=1, device_id=(gx, gy + 1), device_id_type=MESH)
+
+    def tell(sem, cond, x, y):
+        @pl.when(cond)
+        def _():
+            pl.semaphore_signal(sem, inc=1, device_id=(x, y), device_id_type=MESH)
+
+    right, left = lax.rem(gx + 1, nx), lax.rem(gx + last, nx)
+    right2, left2 = lax.rem(gx + 2, nx), lax.rem(gx + last - 1, nx)
+    tell(barrier, gx < last, right, gy)
+    tell(barrier, gx < last - 1, right2, gy)
+    pl.semaphore_signal(barrier, inc=1, device_id=(left, gy), device_id_type=MESH)
+    pl.semaphore_signal(barrier, inc=1, device_id=(left2, gy), device_id_type=MESH)
+    tell(barrier, gy < ny - 1, gx, gy + 1)
 
     low, high = jnp.minimum(gy, 1), jnp.minimum(ny - 1 - gy, 1)
     kind = low + 1 - high
-    pltpu.make_async_copy(tables.at[kind], late.at[0:t_rows], load_sem.at[1]).start()
-    pltpu.make_async_copy(stretch, late.at[t_rows : t_rows + ny], load_sem.at[1]).start()
-    pltpu.make_async_copy(metric, late.at[t_rows + ny : t_rows + 2 * ny], load_sem.at[1]).start()
+    pltpu.make_async_copy(tables.at[kind], late.at[0:t_rows], sems.at[1]).start()
+    pltpu.make_async_copy(stretch, late.at[t_rows : t_rows + ny], sems.at[1]).start()
+    pltpu.make_async_copy(metric, late.at[t_rows + ny : t_rows + 2 * ny], sems.at[1]).start()
 
     place = lax.broadcasted_iota(jnp.int32, (8, width), 0)
 
@@ -134,7 +130,7 @@
     up1, down1 = powers(R1, False), powers(R1, True)
     up2, down2 = powers(R2, False), powers(R2, True)
 
-    pltpu.make_async_copy(vel, f, load_sem.at[0]).wait()
+    pltpu.make_async_copy(vel, f, sems.at[0]).wait()
     step1, step2 = np.float32(R1**8), np.float32(R2**8)
 
     def weighted(c, order, step, base):
@@ -144,7 +140,7 @@
         return jnp.sum(total * base, axis=0, keepdims=True)
 
     rising, falling = list(range(steps)), list(range(steps))[::-1]
-    to_right, to_left = 1 - odd, odd
+    to_right, to_left = 0, 1
     for c in range(comps):
         xs[to_right, c : c + 1] = weighted(c, rising, step1, down1)
         xs[to_right, 8 + c : 9 + c] = weighted(c, rising, step2, down2)
@@ -153,35 +149,42 @@
         xs[to_left, 8 + c : 9 + c] = weighted(c, falling, step2, up2)
         xs[to_left, 16 + c : 17 + c] = f[c, 0:1]
 
-    pl.semaphore_wait(barrier, len(peers) + low + high)
-
-    def send(src, dst, sem, peer):
+    def flag(value):
+        return jnp.minimum(jnp.maximum(value, 0), 1)
+
+    pl.semaphore_wait(barrier, 2 + flag(gx) + flag(gx - 1) + low)
+
+    def send(src, dst, pair, peer):
         return pltpu.make_async_remote_copy(
-            src_ref=src, dst_ref=dst, send_sem=sem.at[0], recv_sem=sem.at[1],
+            src_ref=src, dst_ref=dst, send_sem=sems.at[pair], recv_sem=sems.at[pair + 1],
             device_id=peer, device_id_type=MESH,
         )
 
-    send(xs.at[0], xr.at[0, 0:24], x_sem, (outer, gy)).start()
-    if FAR:
-        send(xs.at[1, 0:16], xr.at[0, 24:40], x_sem, (far_partner, gy)).start()
-    send(xs.at[1], xr.at[1, 0:24], x_sem, (partner, gy)).start()
-    if FAR:
-        send(xs.at[0, 0:16], xr.at[1, 24:40], x_sem, (far_outer, gy)).start()
-
-    pltpu.make_async_copy(late, late, load_sem.at[1]).wait()
+    def send_left():
+        send(xs.at[1], xr.at[1, 0:24], 2, (left, gy)).start()
+
+    def send_left2():
+        send(xs.at[1, 0:16], xr.at[1, 24:40], 2, (left2, gy)).start()
+
+    send(xs.at[0], xr.at[0, 0:24], 2, (right, gy)).start()
+    pl.when(gx > 0)(send_left)
+    send(xs.at[0, 0:16], xr.at[0, 24:40], 2, (right2, gy)).start()
+    pl.when(gx > 1)(send_left2)
+    tell(ready.at[0], gx == last, 0, gy)
+    tell(ready.at[0], gx == last, 1, gy)
+    tell(ready.at[0], gx == last - 1, 0, gy)
+    tell(ready.at[1], gy > 0, gx, gy - 1)
+
+    pltpu.make_async_copy(late, late, sems.at[1]).wait()
     flat = f[...].reshape(comps * rows, width)
     ys[...] = lax.dot_general(
         late[0:8], flat, (((1,), (1,)), ((), ())), precision=HIGHEST,
         preferred_element_type=jnp.float32,
     )
 
-    @pl.when(gy < ny - 1)
-    def _():
-        send(ys, yr.at[0:8], y_sem, (gx, gy + 1)).start()
-
     @pl.when(gy > 0)
     def _():
-        send(ys, yr.at[8:16], y_sem, (gx, gy - 1)).start()
+        send(ys, yr.at[8:16], 4, (gx, gy - 1)).start()
 
     @pl.when(gy == 0)
     def _():
@@ -213,15 +216,27 @@
         u = f[3 * (c // 3)]
         out[c] = own_x[rows:, at] - u * own_x[:rows, at] + along_y(own_y, c)
 
+    @pl.when(gy < ny - 1)
+    def _():
+        pl.semaphore_wait(ready.at[1], 1)
+        send(ys, yr.at[0:8], 4, (gx, gy + 1)).start()
+
+    @pl.when(gx < 2)
+    def _():
+        pl.semaphore_wait(ready.at[0], 2 - gx)
+        send_left2()
+
+    pl.when(gx == 0)(send_left)
+
     inside = low + high == 2
 
     @pl.when(inside)
     def _():
-        send(yr, yr, y_sem, (partner, gy)).wait_recv()
+        send(yr, yr, 4, (right, gy)).wait_recv()
 
     @pl.when(jnp.logical_not(inside))
     def _():
-        send(ys, ys, y_sem, (partner, gy)).wait_recv()
+        send(ys, ys, 4, (right, gy)).wait_recv()
 
     spread = jnp.concatenate([late[8:24], late[24:40]], axis=1)
     beside = lax.dot_general(
@@ -231,17 +246,15 @@
     for c in range(comps):
         out[c] = out[c] + along_y(beside, c)
 
-    send(xr, xr, x_sem, (partner, gy)).wait_recv()
-    left, right = odd, 1 - odd
+    send(xr, xr, 2, (right, gy)).wait_recv()
     far1, far2 = np.float32(R1**rows), np.float32(R2**rows)
-    left1, left2 = xr[left, 0:8], xr[left, 8:16]
-    right1, right2 = xr[right, 0:8], xr[right, 8:16]
-    if FAR:
-        left1, left2 = left1 + far1 * xr[left, 24:32], left2 + far2 * xr[left, 32:40]
-        right1, right2 = right1 + far1 * xr[right, 24:32], right2 + far2 * xr[right, 32:40]
+    left1, left2 = xr[0, 0:8], xr[0, 8:16]
+    right1, right2 = xr[1, 0:8], xr[1, 8:16]
+    left1, left2 = left1 + far1 * xr[0, 24:32], left2 + far2 * xr[0, 32:40]
+    right1, right2 = right1 + far1 * xr[1, 24:32], right2 + far2 * xr[1, 32:40]
     left1, right1 = left1 * np.float32(G1 / R1), right1 * np.float32(-G1 / R1)
     left2, right2 = left2 * np.float32(0.5 * G2 / R2), right2 * np.float32(0.5 * G2 / R2)
-    left_cell, right_cell = xr[left, 16:24], xr[right, 16:24]
+    left_cell, right_cell = xr[0, 16:24], xr[1, 16:24]
     for c in range(comps):
         row = slice(c, c + 1)
         u = f[3 * (c // 3)]
@@ -261,18 +274,15 @@
                 first, second = first - NEAR1 * cell, second + 0.5 * NEAR2 * cell
             out[c, part] = out[c, part] + (second - u[part] * first)
 
-    if FAR:
-        send(xr, xr, x_sem, (partner, gy)).wait_send()
-    else:
-        send(xs, xs, x_sem, (partner, gy)).wait_send()
+    send(xr, xr, 2, (right, gy)).wait_send()
 
     @pl.when(inside)
     def _():
-        send(yr, yr, y_sem, (partner, gy)).wait_send()
+        send(yr, yr, 4, (right, gy)).wait_send()
 
     @pl.when(jnp.logical_not(inside))
     def _():
-        send(ys, ys, y_sem, (partner, gy)).wait_send()
+        send(ys, ys, 4, (right, gy)).wait_send()
 
 
 def solution(mesh):
@@ -306,11 +316,10 @@
                 pltpu.VMEM((tables.shape[1] + 2 * ny, width), f32),
                 pltpu.VMEM((2, 24, width), f32),
                 pltpu.VMEM((8, comps * rows), f32),
-                pltpu.VMEM((2, 40 if FAR else 24, width), f32),
+                pltpu.VMEM((2, 40, width), f32),
                 pltpu.VMEM((16, comps * rows), f32),
-                pltpu.SemaphoreType.DMA((2,)),
-                pltpu.SemaphoreType.DMA((2,)),
-                pltpu.SemaphoreType.DMA((2,)),
+                pltpu.SemaphoreType.DMA((6,)),
+                pltpu.SemaphoreType.REGULAR((2,)),
             ],
             compiler_params=pltpu.CompilerParams(collective_id=0, has_side_effects=True),
         )(

time: 11.9 us -> 10.1 us (0.85)
  the two profiles are of different devices: /device:TPU:96 before, /device:TPU:1 now
where the time goes in v2:
time: 10.1 us
  Pallas kernels  9.38 us (93%)
  local copies, waits for them, and re-layouts  0.66 us (7%)
    pallas_call x1, Pallas kernels, shards(): pl.pallas_call(functools.partial(kernel, nx, ny), out_shape=pltpu.VMEM((c...  9.38 us
    unnamed x1, local copies, waits for them, and re-layouts  0.66 us

profile of v2, /device:TPU:1, one launch (start us, length us, event | category | flops | bytes accessed | tf_op | source)
XLA Modules:
  0.0 10.1 jit_solution(12735966019044329946)
XLA Ops:
  0.0 9.4 %shard_map.46 = f32[6,48,128]{2,1,0:T(8,128)S(1)} custom-call(f32[6,48,128]{2,1,0:T(8,128)} %bitcast.5, f32[3,392,128]{2,1,0:T(8,128)} %constant.2.clone.tables, f32[8,128]{1,0:T(8,128)} %bitcast.6, f32[8,128]{1,0:T(8,128)} %bitcast.7), custom_call_target="tpu_custom_call" | custom-call | tf_op jit(solution)/shard_map/pallas_call | solution.py:309
  9.4 0.7 %copy.6 = f32[2,3,48,128]{3,2,1,0:T(8,128)} copy(f32[2,3,48,128]{3,2,1,0:T(8,128)S(1)} %bitcast.4) | data formatting | bytes 294912
